TPU v7x, 256 devices: a whole 4x4x8 slice. The times are simulated.
256 devices in a mesh: pack: 32 (over y, z), hist: 8 (over x, core).
Axes of the slice: x: 4, y: 4, z: 8, core: 2. Of those that a mesh axis runs over, the one named last changes fastest.
Arguments:
- queries: bfloat16 [32, 4096, 2048], P('pack', 'hist'), may hold values from -0.59765625 to 0.59765625
- keys: bfloat16 [32, 4096, 2048], P('pack', 'hist'), may hold values from -6 to 6
- values: bfloat16 [32, 4096, 2048], P('pack', 'hist'), may hold values from -6 to 6
- gates: bfloat16 [32, 4096, 2048], P('pack', 'hist'), may hold values from -6 to 6
- user_ids: int32 [32, 4096], P('pack', 'hist'), may hold values from 0 to 5, never falling along the last dimension, each value on 1 to 1365 neighbouring positions
- forget_rate: float32 [16], replicated, may hold values from 0.0001 to 0.02
- norm_gain: float32 [2048], replicated, may hold values from 0.1 to 1.9
- w_out: bfloat16 [2048, 2048], P('pack'), may hold values from -0.125 to 0.125
Outputs:
- mixed: bfloat16 [32, 4096, 2048], P('pack', 'hist')
Inputs may be any that keep to these rules, and one draw needn't show every extreme that they name: `user_ids`: in each window user ids never fall along the events; each user holds 1 to 1365 consecutive events, and one user exactly 1365.
All inputs are finite; a program needn't handle non-finite values.
Results may differ from a plain program's by a relative error of at most 0.0061.
Values may be sent and summed in bfloat16 or wider, within the bound.
No kernel may reach another device: no remote copies, remote signals or barrier semaphores. Data moves between devices by JAX's collectives and lax.ppermute only.
A program may use at most 128 MiB of HBM per device.

v0:
```python
import jax
import jax.numpy as jnp
from jax import lax
from jax.sharding import PartitionSpec as P

HEADS = 16
GROUP = 128


def passed_along(array, axis, by):
    size = lax.axis_size(axis)
    pairs = [(i, i + by) for i in range(size) if 0 <= i + by < size]
    return lax.ppermute(array, axis, pairs)


def carried_in(array, axis, combine, identity):
    size, here = (lax.axis_size(axis), lax.axis_index(axis))
    everything = jax.tree.map(lambda part: lax.all_gather(part, axis), array)
    start = jax.tree.map(
        lambda part, zero: jnp.broadcast_to(jnp.asarray(zero, part.dtype), part.shape),
        array,
        identity,
    )

    def hop(k, before):
        reached = k < here
        new = combine(before, jax.tree.map(lambda part: part[k], everything))
        return jax.tree.map(lambda a, b: jnp.where(reached, a, b), new, before)

    return lax.fori_loop(0, size, hop, start)


def combine_states(earlier, later):
    return (earlier[0] * later[0], later[0][:, None, None] * earlier[1] + later[1])


def local(queries, keys, values, gates, user_ids, forget_rate, norm_gain, w_out):
    length = queries.shape[1]
    width = queries.shape[2]
    head_dim = width // HEADS
    blocks = length // GROUP
    log_decay = jnp.log1p(-forget_rate)
    users = user_ids[0]
    before = passed_along(users[length - 1 :], "hist", 1)
    prior = jnp.concatenate([before, users[:-1]])
    place_all = jnp.arange(length, dtype=jnp.int32)
    forced = jnp.logical_and(lax.axis_index("hist") == 0, place_all == 0)
    starts = jnp.logical_or(users != prior, forced).astype(jnp.int32)
    seg = users.reshape(blocks, GROUP)
    start_blk = starts.reshape(blocks, GROUP)
    q_blk = queries[0].reshape(blocks, GROUP, HEADS, head_dim)
    k_blk = keys[0].reshape(blocks, GROUP, HEADS, head_dim)
    v_blk = values[0].reshape(blocks, GROUP, HEADS, head_dim)
    place = jnp.arange(GROUP, dtype=jnp.int32)
    diff = place[:, None] - place[None, :]
    causal = diff >= 0
    lag = jnp.where(causal, diff, 0).astype(jnp.float32)
    decay = jnp.exp(lag[None] * log_decay[:, None, None])
    mask = jnp.logical_and(seg[:, :, None] == seg[:, None, :], causal[None])
    scores = jnp.einsum("nthd,nshd->nhts", q_blk, k_blk, preferred_element_type=jnp.float32)
    weights = jnp.where(mask[:, None], scores * decay[None], 0.0).astype(jnp.bfloat16)
    inner = jnp.einsum("nhts,nshd->nthd", weights, v_blk, preferred_element_type=jnp.float32)
    tail = jnp.exp((GROUP - 1 - place).astype(jnp.float32)[None, :] * log_decay[:, None])
    keep_rows = (seg == seg[:, -1:]).astype(jnp.float32)
    scaled = (k_blk * (keep_rows[:, :, None] * tail.T[None])[..., None]).astype(jnp.bfloat16)
    own = jnp.einsum("nshd,nshe->nhde", scaled, v_blk, preferred_element_type=jnp.float32)
    any_start = jnp.max(start_blk, axis=1) > 0
    keep = jnp.where(any_start[:, None], 0.0, jnp.exp(GROUP * log_decay)[None, :])

    def advance(state, item):
        keep_c, own_c = item
        return (keep_c[:, None, None] * state + own_c, state)

    zero_state = jnp.zeros((HEADS, head_dim, head_dim), jnp.float32)
    local_final, local_enter = lax.scan(advance, zero_state, (keep, own))
    keep_before = jnp.cumprod(
        jnp.concatenate([jnp.ones((1, HEADS), jnp.float32), keep[:-1]], axis=0), axis=0
    )
    keep_device = keep_before[-1] * keep[-1]
    identity = (
        jnp.ones((HEADS,), jnp.float32),
        jnp.zeros((HEADS, head_dim, head_dim), jnp.float32),
    )
    incoming = carried_in((keep_device, local_final), "hist", combine_states, identity)[1]
    entering = (local_enter + keep_before[:, :, None, None] * incoming[None]).astype(jnp.bfloat16)
    open_run = (jnp.cumsum(start_blk, axis=1) == 0).astype(jnp.float32)
    reach = jnp.exp((place + 1).astype(jnp.float32)[:, None] * log_decay[None, :])
    factor = open_run[:, :, None] * reach[None]
    carried = (
        jnp.einsum("nthd,nhde->nthe", q_blk, entering, preferred_element_type=jnp.float32)
        * factor[..., None]
    )
    retained = (inner + carried).reshape(length, HEADS, head_dim)
    mean = jnp.mean(retained, axis=2, keepdims=True)
    centred = retained - mean
    variance = jnp.mean(centred * centred, axis=2, keepdims=True)
    normed = (centred * lax.rsqrt(variance + 1e-05)).reshape(length, width) * norm_gain
    gated = (jax.nn.silu(gates[0].astype(jnp.float32)) * normed).astype(jnp.bfloat16)
    mixed = jnp.dot(
        gated, lax.all_gather(w_out, "pack", axis=0, tiled=True), preferred_element_type=jnp.float32
    ).astype(jnp.bfloat16)
    return mixed[None]


def solution(mesh):
    in_specs = (
        P("pack", "hist", None),
        P("pack", "hist", None),
        P("pack", "hist", None),
        P("pack", "hist", None),
        P("pack", "hist"),
        P(),
        P(),
        P("pack", None),
    )
    out_specs = P("pack", "hist", None)
    return jax.shard_map(local, mesh=mesh, in_specs=in_specs, out_specs=out_specs, check_vma=False)
```

profile of v0, /device:TPU:1, one launch (start us, length us, event | category | flops | bytes accessed | tf_op | source)
XLA Modules:
  0.0 219.2 jit_solution(17431535320970974348)
XLA Ops:
  6.5 0.0 all-gather.7.cloned.1.call-start
  6.5 1.2 slice.26
  7.8 4.5 %collective-permute-start = (s32[1]{0:T(128)}, s32[1]{0:T(128)}, u32[]{:S(2)}, u32[]{:S(2)}) collective-permute-start(s32[1]{0:T(128)} %bitcast.4), channel_id=1, source_target_pairs={{0,1},{1,2},{2,3},{3,4},{4,5},{5,6},{6,7},{8,9},{9,10},{10,11},{11... | collective-permute-start | bytes 20 | tf_op jit(solution)/shard_map/ppermute | solution.py:13
  12.3 0.9 slice_reduce_fusion
  13.2 0.8 compare_convert_fusion.1
  13.9 0.7 multiply_exponential_fusion.3
  14.6 3.5 %copy.41 = bf16[64,8,16,128]{3,2,1,0:T(8,128)(2,1)} copy(bf16[64,8,16,128]{3,1,2,0:T(8,128)(2,1)} %bitcast.105) | data formatting | bytes 4194304
  18.1 0.0 copy-start.3
  18.1 3.5 %copy.26 = bf16[4,128,16,128]{1,3,2,0:T(8,128)(2,1)S(1)} copy(bf16[4,128,16,128]{3,2,1,0:T(8,128)(2,1)} %bitcast.100) | data formatting | bytes 4194304 | tf_op jit(solution)/shard_map/reshape;squeeze | solution.py:52
  21.6 0.0 copy-start.1
  21.6 4.3 %copy.42 = bf16[64,8,16,128]{3,2,1,0:T(8,128)(2,1)} copy(bf16[64,8,16,128]{3,1,2,0:T(8,128)(2,1)} %bitcast.106) | data formatting | bytes 4194304
  25.9 0.1 multiply_exponential_fusion.1
  26.0 0.0 collective-permute-done
  26.0 0.0 copy-done.3
  26.0 0.8 fusion.31
  26.8 0.3 reduce_window_sum.11
  27.2 0.1 broadcast_select_fusion
  27.2 4.3 %fusion.10 = f32[4,16,128,128]{3,2,1,0:T(8,128)} fusion(bf16[4,128,16,128]{1,3,2,0:T(8,128)(2,1)S(1)} %copy.26, f32[4,128,16]{1,2,0:T(8,128)S(1)} %get-tuple-element.195, bf16[4,128,16,128]{3,2,1,0:T(8,128)(2,1)} %bitcast.98), kind=kOutput, calls=%fused_computation.25 | convolution fusion | flops 271581184 | bytes 8421376 | tf_op jit(solution)/shard_map/nshd,nshe->nhde/dot_general | solution.py:66
  31.6 0.0 copy-done.1
  31.6 10.0 %while.29 = (s32[]{:T(128)}, f32[16,128,128]{2,1,0:T(8,128)S(1)}, f32[4,16,128,128]{3,2,1,0:T(8,128)}, f32[4,16]{1,0:T(4,128)S(1)}, f32[4,16,128,128]{3,2,1,0:T(8,128)}) while((s32[]{:T(128)}, f32[16,128,128]{2,1,0:T(8,128)S(1)}, f32[4,16,128,128]{3,2,1,0:T(8,128)}, f32[4,16]{1,0:T(4,128)S(1)}, ...), condition=%wide.region_2.3_spmd.clone.clone, body=%wide.region_1.2_spmd.clone.sunk.clone | while | flops 1048579 | bytes 5243664 | solution.py:75
  31.6 1.1 bitcast_dynamic-update-slice_fusion.3
  32.6 1.4 bitcast_add_fusion.4
  34.1 1.1 bitcast_dynamic-update-slice_fusion.3
  35.1 1.4 bitcast_add_fusion.4
  36.6 1.1 bitcast_dynamic-update-slice_fusion.3
  37.7 1.4 bitcast_add_fusion.4
  39.1 1.1 bitcast_dynamic-update-slice_fusion.3
  40.2 1.4 bitcast_add_fusion.4
  41.6 0.0 copy-start
  41.6 1.0 copy-done
  42.6 0.0 all-gather.7.cloned.1.call-update
  42.6 0.0 all-gather.5.cloned.1.call-start
  42.6 0.7 all-gather.5.cloned.1.call-update
  43.4 2.2 %copy.40 = bf16[64,8,16,128]{3,2,1,0:T(8,128)(2,1)S(1)} copy(bf16[64,8,16,128]{3,1,2,0:T(8,128)(2,1)} %bitcast.107) | data formatting | bytes 4194304
  45.6 0.1 compare_and_fusion
  45.8 1.2 multiply_exponential_fusion
  46.9 6.8 %fusion.17 = f32[4,16,128,128]{2,3,1,0:T(8,128)} fusion(bf16[4,128,16,128]{3,2,1,0:T(8,128)(2,1)} %bitcast.99, bf16[4,128,16,128]{1,3,2,0:T(8,128)(2,1)} %copy-done.1, f32[16,128,128]{2,1,0:T(8,128)} %multiply_exponential_fusion, pred[4,128,128]{2,1,0:T(8,128)(4,1)S(1)} %compare_and_fusion, bf16[4,128,16,128]{3,2,1,0:T(8,128)(2,1)S(1)} %bitcast.96), kind=kOutput, calls=%fused_computation.31 | convolution fusion | flops 540016640 | bytes 11599872 | tf_op jit(solution)/shard_map/nhts,nshd->nthd/dot_general | solution.py:62
  53.8 9.5 %all-gather.1 = f32[8,1,16]{2,1,0:T(1,128)S(1)} all-gather(f32[1,1,16]{2,1,0:T(1,128)S(1)} %multiply_bitcast_fusion), channel_id=1, replica_groups=mesh['pack'=32,'hist'=8] {'hist'}, dimensions={0}, use_global_device_ids=true | all-gather | bytes 576 | tf_op jit(solution)/shard_map/all_gather | solution.py:18
  63.3 34.2 %all-gather.7.cloned.1.call-done = f32[128,128,128]{2,1,0:T(8,128)} async-done(((f32[16,128,128]{2,1,0:T(8,128)}), f32[128,128,128]{2,1,0:T(8,128)}) %all-gather.7.cloned.1.call-update) | async-done | bytes 8388624 | tf_op jit(solution)/shard_map/all_gather | solution.py:18
  97.5 11.9 %while.30 = (s32[]{:T(128)}, f32[16,128,128]{2,1,0:T(8,128)S(1)}, s32[]{:T(128)}, f32[8,16]{1,0:T(8,128)S(1)}, f32[8,16,128,128]{3,2,1,0:T(8,128)}) while((s32[]{:T(128)}, f32[16,128,128]{2,1,0:T(8,128)S(1)}, s32[]{:T(128)}, f32[8,16]{1,0:T(8,128)S(1)}, f32[8,16,128,128]{3,2,1,0:T(8,128)}) %tuple.71), condition=%wide.region_5.6_spmd.clone.clone, body=%wide.region_4.5_spmd.clone.sunk.clone | while | flops 1048580 | bytes 3146009 | solution.py:30
  97.5 1.5 fusion.41
  99.0 1.5 fusion.41
  100.5 1.5 fusion.41
  102.0 1.5 fusion.41
  103.5 1.5 fusion.41
  105.0 1.5 fusion.41
  106.5 1.5 fusion.41
  108.0 1.5 fusion.41
  109.5 7.4 %fusion.33 = (f32[4,128,16]{1,2,0:T(8,128)S(1)}, f32[4,128,16,128]{1,3,2,0:T(8,128)}) fusion(f32[4,128,16]{1,2,0:T(8,128)S(1)} %get-tuple-element.194, bf16[4,128,16,128]{3,2,1,0:T(8,128)(2,1)S(1)} %bitcast.97, f32[4,16,128,128]{3,2,1,0:T(8,128)} %get-tuple-element.127, f32[16,128,128]{2,1,0:T(8,128)S(1)} %get-tuple-element.129, ...), kind=kOutput, calls=%fused_computation.66 | convolution fusion | flops 274718720 | bytes 15794432 | tf_op jit(solution)/shard_map/nthd,nhde->nthe/dot_general | solution.py:90
  116.9 0.1 copy.36
  117.0 5.4 %copy.30 = f32[4,128,16,128]{3,2,1,0:T(8,128)} copy(f32[4,128,16,128]{1,3,2,0:T(8,128)} %get-tuple-element.193) | data formatting | bytes 8388608 | tf_op jit(solution)/shard_map/add | solution.py:93
  122.4 3.0 %multiply_reduce_fusion = f32[4,128,16]{1,2,0:T(8,128)S(1)} fusion(f32[4,128,16,128]{1,3,2,0:T(8,128)} %get-tuple-element.193, f32[4,128,16]{1,2,0:T(8,128)S(1)} %broadcast_multiply_fusion), kind=kLoop, calls=%fused_computation.18 | loop fusion | flops 3137536 | bytes 4259840 | tf_op jit(solution)/shard_map/reduce_sum | solution.py:96
  125.5 0.1 copy.37
  125.6 71.4 %all-gather.5.cloned.1.call-done = bf16[2048,2048]{1,0:T(8,128)(2,1)} async-done(((bf16[64,2048]{1,0:T(8,128)(2,1)}), bf16[2048,2048]{1,0:T(8,128)(2,1)}) %all-gather.5.cloned.1.call-update) | async-done | bytes 8388624 | tf_op jit(solution)/shard_map/all_gather | solution.py:100
  197.1 0.0 copy-start.2
  197.1 0.0 copy-start.4
  197.1 0.0 copy-start.5
  197.1 1.1 mul.221
  198.2 1.1 sub.57
  199.3 0.0 copy-done.2
  199.4 0.6 copy-done.4
  199.9 0.0 copy-done.5
  199.9 12.4 %fusion.9 = bf16[1,512,2048]{2,1,0:T(8,128)(2,1)} fusion(bf16[2048,2048]{1,0:T(8,128)(2,1)} %all-gather.5.cloned.1.call-done, f32[64,8,16,128]{3,2,1,0:T(8,128)S(1)} %bitcast.102, f32[64,8,16,128]{3,2,1,0:T(8,128)S(1)} %bitcast.103, f32[64,8,16,128]{3,2,1,0:T(8,128)S(1)} %bitcast.101, bf16[1,512,2048]{2,1,0:T(8,128)(2,1)S(1)} %copy-done.4, ...), kind=kOutput, calls=%fused_computation.24 | convolution fusion | flops 4306501632 | bytes 25174016 | tf_op jit(solution)/shard_map/dot_general | solution.py:99
  (26 shorter events, 0.2 us)
Async XLA Ops:
  6.5 91.0 %all-gather.7.cloned.1.call-start = ((), (), s32[]{:S(2)}) async-start(), calls=%async_computation.1 | async-start | bytes 9437184 | tf_op jit(solution)/shard_map/all_gather | solution.py:18
  7.8 18.2 %collective-permute-start = (s32[1]{0:T(128)}, s32[1]{0:T(128)}, u32[]{:S(2)}, u32[]{:S(2)}) collective-permute-start(s32[1]{0:T(128)} %bitcast.4), channel_id=1, source_target_pairs={{0,1},{1,2},{2,3},{3,4},{4,5},{5,6},{6,7},{8,9},{9,10},{10,11},{11... | collective-permute-start | bytes 20 | tf_op jit(solution)/shard_map/ppermute | solution.py:13
  18.1 7.9 %copy-start.3 = (s32[1,512]{1,0:T(1,128)S(1)}, s32[1,512]{1,0:T(1,128)}, u32[]{:S(2)}) copy-start(s32[1,512]{1,0:T(1,128)} %param.16) | copy-start | bytes 6148
  21.6 10.0 %copy-start.1 = (bf16[4,128,16,128]{1,3,2,0:T(8,128)(2,1)}, bf16[4,128,16,128]{1,3,2,0:T(8,128)(2,1)S(1)}, u32[]{:S(2)}) copy-start(bf16[4,128,16,128]{1,3,2,0:T(8,128)(2,1)S(1)} %copy.26) | copy-start | bytes 6291460
  41.6 1.0 copy-start
  42.6 154.5 %all-gather.5.cloned.1.call-start = ((), (), s32[]{:S(2)}) async-start(), calls=%async_computation | async-start | bytes 8650752 | tf_op jit(solution)/shard_map/all_gather | solution.py:100
  197.1 2.3 %copy-start.2 = (f32[4,128,16,128]{3,2,1,0:T(8,128)S(1)}, f32[4,128,16,128]{3,2,1,0:T(8,128)}, u32[]{:S(2)}) copy-start(f32[4,128,16,128]{3,2,1,0:T(8,128)} %copy.30) | copy-start | bytes 12582916
  197.1 2.9 %copy-start.4 = (bf16[1,512,2048]{2,1,0:T(8,128)(2,1)S(1)}, bf16[1,512,2048]{2,1,0:T(8,128)(2,1)}, u32[]{:S(2)}) copy-start(bf16[1,512,2048]{2,1,0:T(8,128)(2,1)} %param.15) | copy-start | bytes 6291460
  197.1 2.9 %copy-start.5 = (f32[2048]{0:T(1024)S(1)}, f32[2048]{0:T(1024)}, u32[]{:S(2)}) copy-start(f32[2048]{0:T(1024)} %param.18) | copy-start | bytes 24580
Sparse Core Ops, SparseCore 0:
  42.7 54.7 all-gather.6
  100.1 96.9 all-gather.4
where the time goes:
time: 220 us; the launch traced here: 219 us
  waiting for transfers between devices  106 us (48%)
  matrix products  30.9 us (14%)
  other arithmetic  28.8 us (13%)
  local copies, waits for them, and re-layouts  25.2 us (11%)
  between operations  13.6 us (6%)
  blocking collectives  9.47 us (4%)
  starting transfers between devices  4.53 us (2%)
    all_gather x1, waiting for transfers between devices, local(): lax.all_gather(w_out, 'pack', axis=0, tiled=True)  71.4 us
    all_gather x1, waiting for transfers between devices, carried_in(): everything = jax.tree.map(lambda part: lax.all_gather(part, axis), array)  34.2 us
    dot_general x1, matrix products, local(): jnp.dot(gated, lax.all_gather(w_out, 'pack', axis=0, tiled=True), preferr...  12.4 us
    select_n x8, other arithmetic, hop(): return jax.tree.map(lambda a, b: jnp.where(reached, a, b), new, before)  11.7 us
    unnamed x15, local copies, waits for them, and re-layouts  11.6 us
    all_gather x1, blocking collectives, carried_in(): everything = jax.tree.map(lambda part: lax.all_gather(part, axis), array)  9.47 us
    dot_general x1, matrix products, local(): jnp.einsum('nthd,nhde->nthe', q_blk, entering, preferred_element_type=jnp...  7.41 us
    dot_general x1, matrix products, local(): jnp.einsum('nhts,nshd->nthd', weights, v_blk, preferred_element_type=jnp....  6.81 us
  transfers between devices with their start and end apart: 3, of which 2 were waited for; matrix products, arithmetic and copies ran while one was open for 24% of the time, Pallas kernels for 0%

commit v1 on v0

--- a/solution.py
+++ b/solution.py
@@ -96,9 +96,19 @@
     variance = jnp.mean(centred * centred, axis=2, keepdims=True)
     normed = (centred * lax.rsqrt(variance + 1e-05)).reshape(length, width) * norm_gain
     gated = (jax.nn.silu(gates[0].astype(jnp.float32)) * normed).astype(jnp.bfloat16)
-    mixed = jnp.dot(
-        gated, lax.all_gather(w_out, "pack", axis=0, tiled=True), preferred_element_type=jnp.float32
-    ).astype(jnp.bfloat16)
+
+    def replace_unit(z):
+        buffer = []
+        for _ in range(lax.axis_size("pack")):
+            buffer.append(z)
+        clean = jnp.concatenate(
+            lax.all_to_all(jnp.stack(buffer, 0), axis_name="pack", split_axis=0, concat_axis=0), 0
+        )
+        return clean
+
+    mixed = jnp.dot(gated, replace_unit(w_out), preferred_element_type=jnp.float32).astype(
+        jnp.bfloat16
+    )
     return mixed[None]
 
 

time: 220 us -> 280 us (1.27)
  the two profiles are of different devices: /device:TPU:1 before, /device:TPU:107 now
where the time goes in v1:
time: 280 us; the launch traced here: 279 us
  waiting for transfers between devices  136 us (49%)
  local copies, waits for them, and re-layouts  46.8 us (17%)
  matrix products  31.9 us (11%)
  other arithmetic  28.8 us (10%)
  between operations  13.6 us (5%)
  starting transfers between devices  13.5 us (5%)
  blocking collectives  8.44 us (3%)
    all_to_all x1, waiting for transfers between devices, replace_unit(): lax.all_to_all(jnp.stack(buffer, 0), axis_name='pack', split_axis=0, conc...  116 us
    all_gather x1, waiting for transfers between devices, carried_in(): everything = jax.tree.map(lambda part: lax.all_gather(part, axis), array)  19.6 us
    dot_general x1, matrix products, local(): jnp.dot(gated, replace_unit(w_out), preferred_element_type=jnp.float32)  13.4 us
    select_n x8, other arithmetic, hop(): return jax.tree.map(lambda a, b: jnp.where(reached, a, b), new, before)  11.7 us
    unnamed x15, local copies, waits for them, and re-layouts  11.2 us
    all_to_all x1, starting transfers between devices, replace_unit(): lax.all_to_all(jnp.stack(buffer, 0), axis_name='pack', split_axis=0, conc...  9.84 us
    all_gather x1, blocking collectives, carried_in(): everything = jax.tree.map(lambda part: lax.all_gather(part, axis), array)  8.44 us
    mul x2, local copies, waits for them, and re-layouts, local(): centred * lax.rsqrt(variance + 1e-05)  7.59 us
  transfers between devices with their start and end apart: 3, of which 2 were waited for; matrix products, arithmetic and copies ran while one was open for 27% of the time, Pallas kernels for 0%

profile of v1, /device:TPU:107, one launch (start us, length us, event | category | flops | bytes accessed | tf_op | source)
XLA Modules:
  0.0 278.9 jit_solution(6878262342603989463)
XLA Ops:
  6.5 0.0 all-gather.4.cloned.1.call-start
  6.5 1.3 slice.26
  7.8 3.7 %collective-permute-start = (s32[1]{0:T(128)}, s32[1]{0:T(128)}, u32[]{:S(2)}, u32[]{:S(2)}) collective-permute-start(s32[1]{0:T(128)} %bitcast.2), channel_id=1, source_target_pairs={{0,1},{1,2},{2,3},{3,4},{4,5},{5,6},{6,7},{8,9},{9,10},{10,11},{11... | collective-permute-start | bytes 20 | tf_op jit(solution)/shard_map/ppermute | solution.py:13
  11.5 0.9 slice_reduce_fusion
  12.4 0.7 multiply_exponential_fusion.3
  13.1 0.8 compare_convert_fusion.1
  13.8 3.5 %copy.41 = bf16[64,8,16,128]{3,2,1,0:T(8,128)(2,1)} copy(bf16[64,8,16,128]{3,1,2,0:T(8,128)(2,1)} %bitcast.79) | data formatting | bytes 4194304
  17.4 0.0 copy-start.3
  17.4 3.5 %copy.26 = bf16[4,128,16,128]{1,3,2,0:T(8,128)(2,1)S(1)} copy(bf16[4,128,16,128]{3,2,1,0:T(8,128)(2,1)} %bitcast.77) | data formatting | bytes 4194304 | tf_op jit(solution)/shard_map/reshape;squeeze | solution.py:52
  20.8 0.0 copy-start.1
  20.8 4.3 %copy.42 = bf16[64,8,16,128]{3,2,1,0:T(8,128)(2,1)} copy(bf16[64,8,16,128]{3,1,2,0:T(8,128)(2,1)} %bitcast.80) | data formatting | bytes 4194304
  25.1 0.1 multiply_exponential_fusion.1
  25.2 0.0 collective-permute-done
  25.2 0.0 copy-done.3
  25.2 0.8 fusion.30
  26.0 0.3 reduce_window_sum.11
  26.4 0.1 broadcast_select_fusion
  26.4 4.3 %fusion.9 = f32[4,16,128,128]{3,2,1,0:T(8,128)} fusion(bf16[4,128,16,128]{1,3,2,0:T(8,128)(2,1)S(1)} %copy.26, f32[4,128,16]{1,2,0:T(8,128)S(1)} %get-tuple-element.195, bf16[4,128,16,128]{3,2,1,0:T(8,128)(2,1)} %bitcast.75), kind=kOutput, calls=%fused_computation.22 | convolution fusion | flops 271581184 | bytes 8421376 | tf_op jit(solution)/shard_map/nshd,nshe->nhde/dot_general | solution.py:66
  30.8 0.0 copy-done.1
  30.8 0.0 copy-start.2
  30.8 10.1 %while.29 = (s32[]{:T(128)}, f32[16,128,128]{2,1,0:T(8,128)S(1)}, f32[4,16,128,128]{3,2,1,0:T(8,128)}, f32[4,16]{1,0:T(4,128)S(1)}, f32[4,16,128,128]{3,2,1,0:T(8,128)}) while((s32[]{:T(128)}, f32[16,128,128]{2,1,0:T(8,128)S(1)}, f32[4,16,128,128]{3,2,1,0:T(8,128)}, f32[4,16]{1,0:T(4,128)S(1)}, ...), condition=%wide.region_2.3_spmd.clone.clone, body=%wide.region_1.2_spmd.clone.sunk.clone | while | flops 1048579 | bytes 5243164 | solution.py:75
  30.8 1.1 bitcast_dynamic-update-slice_fusion.3
  31.9 1.4 bitcast_add_fusion.4
  33.3 1.0 bitcast_dynamic-update-slice_fusion.3
  34.4 1.4 bitcast_add_fusion.4
  35.8 1.1 bitcast_dynamic-update-slice_fusion.3
  36.9 1.4 bitcast_add_fusion.4
  38.4 1.1 bitcast_dynamic-update-slice_fusion.3
  39.4 1.4 bitcast_add_fusion.4
  40.9 0.0 copy-start
  40.9 1.0 copy-done
  41.9 0.0 all-gather.4.cloned.1.call-update
  41.9 0.0 copy-done.2
  41.9 4.3 %stack.2 = bf16[32,64,2048]{2,1,0:T(8,128)(2,1)} broadcast(bf16[64,2048]{1,0:T(8,128)(2,1)S(1)} %copy-done.2), dimensions={1,2} | broadcast | bytes 8650752 | tf_op jit(solution)/shard_map/stack | solution.py:105
  46.2 9.8 %all-to-all-start = ((bf16[32,64,2048]{2,1,0:T(8,128)(2,1)}), bf16[32,64,2048]{2,1,0:T(8,128)(2,1)}, u32[]{:S(2)}, u32[]{:S(2)}) async-start(bf16[32,64,2048]{2,1,0:T(8,128)(2,1)} %stack.2), calls=%async_computation | async-start | bytes 16777216 | tf_op jit(solution)/shard_map/all_to_all | solution.py:105
  56.0 2.4 copy.40
  58.4 0.1 compare_and_fusion
  58.6 1.2 multiply_exponential_fusion
  59.8 6.9 %fusion.16 = f32[4,16,128,128]{2,3,1,0:T(8,128)} fusion(bf16[4,128,16,128]{3,2,1,0:T(8,128)(2,1)} %bitcast.76, bf16[4,128,16,128]{1,3,2,0:T(8,128)(2,1)} %copy-done.1, f32[16,128,128]{2,1,0:T(8,128)} %multiply_exponential_fusion, pred[4,128,128]{2,1,0:T(8,128)(4,1)S(1)} %compare_and_fusion, bf16[4,128,16,128]{3,2,1,0:T(8,128)(2,1)S(1)} %bitcast.73), kind=kOutput, calls=%fused_computation.28 | convolution fusion | flops 540016640 | bytes 11599872 | tf_op jit(solution)/shard_map/nhts,nshd->nthd/dot_general | solution.py:62
  66.7 8.4 %all-gather.1 = f32[8,1,16]{2,1,0:T(1,128)S(1)} all-gather(f32[1,1,16]{2,1,0:T(1,128)S(1)} %multiply_bitcast_fusion), channel_id=1, replica_groups=mesh['pack'=32,'hist'=8] {'hist'}, dimensions={0}, use_global_device_ids=true | all-gather | bytes 576 | tf_op jit(solution)/shard_map/all_gather | solution.py:18
  75.2 19.6 %all-gather.4.cloned.1.call-done = f32[128,128,128]{2,1,0:T(8,128)} async-done(((f32[16,128,128]{2,1,0:T(8,128)}), f32[128,128,128]{2,1,0:T(8,128)}) %all-gather.4.cloned.1.call-update) | async-done | bytes 8388624 | tf_op jit(solution)/shard_map/all_gather | solution.py:18
  94.8 12.0 %while.30 = (s32[]{:T(128)}, f32[16,128,128]{2,1,0:T(8,128)S(1)}, s32[]{:T(128)}, f32[8,16]{1,0:T(8,128)S(1)}, f32[8,16,128,128]{3,2,1,0:T(8,128)}) while((s32[]{:T(128)}, f32[16,128,128]{2,1,0:T(8,128)S(1)}, s32[]{:T(128)}, f32[8,16]{1,0:T(8,128)S(1)}, f32[8,16,128,128]{3,2,1,0:T(8,128)}) %tuple.69), condition=%wide.region_5.6_spmd.clone.clone, body=%wide.region_4.5_spmd.clone.sunk.clone | while | flops 1048580 | bytes 3146017 | solution.py:30
  94.8 1.5 fusion.40
  96.3 1.5 fusion.40
  97.8 1.5 fusion.40
  99.3 1.5 fusion.40
  100.8 1.5 fusion.40
  102.3 1.5 fusion.40
  103.8 1.5 fusion.40
  105.3 1.5 fusion.40
  106.8 7.3 %fusion.32 = (f32[4,128,16]{1,2,0:T(8,128)S(1)}, f32[4,128,16,128]{1,3,2,0:T(8,128)}) fusion(f32[4,128,16]{1,2,0:T(8,128)S(1)} %get-tuple-element.194, bf16[4,128,16,128]{3,2,1,0:T(8,128)(2,1)S(1)} %bitcast.74, f32[4,16,128,128]{3,2,1,0:T(8,128)} %get-tuple-element.127, f32[16,128,128]{2,1,0:T(8,128)S(1)} %get-tuple-element.129, ...), kind=kOutput, calls=%fused_computation.63 | convolution fusion | flops 274718720 | bytes 15794432 | tf_op jit(solution)/shard_map/nthd,nhde->nthe/dot_general | solution.py:90
  114.1 5.4 %copy.30 = f32[4,128,16,128]{3,2,1,0:T(8,128)} copy(f32[4,128,16,128]{1,3,2,0:T(8,128)} %get-tuple-element.193) | data formatting | bytes 8388608 | tf_op jit(solution)/shard_map/add | solution.py:93
  119.5 4.9 %reshape.270 = f32[1,512,2048]{2,1,0:T(8,128)} reshape(f32[4,128,16,128]{3,2,1,0:T(8,128)} %copy.30) | data formatting | bytes 8388608 | tf_op jit(solution)/shard_map/reshape | solution.py:93
  124.4 0.1 copy.36
  124.5 3.0 %multiply_reduce_fusion = f32[4,128,16]{1,2,0:T(8,128)S(1)} fusion(f32[4,128,16,128]{1,3,2,0:T(8,128)} %get-tuple-element.193, f32[4,128,16]{1,2,0:T(8,128)S(1)} %broadcast_multiply_fusion), kind=kLoop, calls=%fused_computation.15 | loop fusion | flops 3137536 | bytes 4259840 | tf_op jit(solution)/shard_map/reduce_sum | solution.py:96
  127.6 0.1 copy.37
  127.7 2.6 sub.64
  130.3 4.9 %sub.65 = f32[1,512,2048]{2,1,0:T(8,128)} reshape(f32[512,16,128]{2,1,0:T(8,128)} %sub.64) | data formatting | bytes 8388608 | tf_op jit(solution)/shard_map/sub | solution.py:95
  135.2 2.6 mul.237
  137.7 5.0 %mul.238 = f32[1,512,2048]{2,1,0:T(8,128)} reshape(f32[512,16,128]{2,1,0:T(8,128)} %mul.237) | data formatting | bytes 8388608 | tf_op jit(solution)/shard_map/mul | solution.py:97
  142.8 115.9 %all-to-all-done = bf16[32,64,2048]{2,1,0:T(8,128)(2,1)} async-done(((bf16[32,64,2048]{2,1,0:T(8,128)(2,1)}), bf16[32,64,2048]{2,1,0:T(8,128)(2,1)}, u32[]{:S(2)}, u32[]{:S(2)}) %all-to-all-start) | async-done | bytes 8388640 | tf_op jit(solution)/shard_map/all_to_all | solution.py:105
  258.6 0.0 copy-done.4
  258.7 0.0 copy-done.5
  258.7 13.4 %fusion.8 = bf16[1,512,2048]{2,1,0:T(8,128)(2,1)} fusion(bf16[2048,2048]{1,0:T(8,128)(2,1)} %bitcast.12, f32[1,512,2048]{2,1,0:T(8,128)} %mul.238, f32[1,512,2048]{2,1,0:T(8,128)} %reshape.270, f32[1,512,2048]{2,1,0:T(8,128)} %sub.65, bf16[1,512,2048]{2,1,0:T(8,128)(2,1)S(1)} %copy-done.4, f32[2048]{0:T(1024)S(1)} %copy-done.5), kind=kOutput, calls=%fused_computation.21 | convolution fusion | flops 4306501632 | bytes 25174016 | tf_op jit(solution)/shard_map/dot_general | solution.py:109
  (28 shorter events, 0.2 us)
Async XLA Ops:
  6.5 88.3 %all-gather.4.cloned.1.call-start = ((), (), s32[]{:S(2)}) async-start(), calls=%async_computation.1 | async-start | bytes 9437184 | tf_op jit(solution)/shard_map/all_gather | solution.py:18
  7.8 17.4 %collective-permute-start = (s32[1]{0:T(128)}, s32[1]{0:T(128)}, u32[]{:S(2)}, u32[]{:S(2)}) collective-permute-start(s32[1]{0:T(128)} %bitcast.2), channel_id=1, source_target_pairs={{0,1},{1,2},{2,3},{3,4},{4,5},{5,6},{6,7},{8,9},{9,10},{10,11},{11... | collective-permute-start | bytes 20 | tf_op jit(solution)/shard_map/ppermute | solution.py:13
  17.4 7.9 %copy-start.3 = (s32[1,512]{1,0:T(1,128)S(1)}, s32[1,512]{1,0:T(1,128)}, u32[]{:S(2)}) copy-start(s32[1,512]{1,0:T(1,128)} %param.16) | copy-start | bytes 6148
  20.8 9.9 %copy-start.1 = (bf16[4,128,16,128]{1,3,2,0:T(8,128)(2,1)}, bf16[4,128,16,128]{1,3,2,0:T(8,128)(2,1)S(1)}, u32[]{:S(2)}) copy-start(bf16[4,128,16,128]{1,3,2,0:T(8,128)(2,1)S(1)} %copy.26) | copy-start | bytes 6291460
  30.8 11.1 %copy-start.2 = (bf16[64,2048]{1,0:T(8,128)(2,1)S(1)}, bf16[64,2048]{1,0:T(8,128)(2,1)}, u32[]{:S(2)}) copy-start(bf16[64,2048]{1,0:T(8,128)(2,1)} %param.19) | copy-start | bytes 786436
  40.9 1.0 copy-start
  46.2 212.5 %all-to-all-start = ((bf16[32,64,2048]{2,1,0:T(8,128)(2,1)}), bf16[32,64,2048]{2,1,0:T(8,128)(2,1)}, u32[]{:S(2)}, u32[]{:S(2)}) async-start(bf16[32,64,2048]{2,1,0:T(8,128)(2,1)} %stack.2), calls=%async_computation | async-start | bytes 16777216 | tf_op jit(solution)/shard_map/all_to_all | solution.py:105
  137.7 120.9 %copy-start.4 = (bf16[1,512,2048]{2,1,0:T(8,128)(2,1)S(1)}, bf16[1,512,2048]{2,1,0:T(8,128)(2,1)}, u32[]{:S(2)}) copy-start(bf16[1,512,2048]{2,1,0:T(8,128)(2,1)} %param.15) | copy-start | bytes 6291460
  137.7 120.9 %copy-start.5 = (f32[2048]{0:T(1024)S(1)}, f32[2048]{0:T(1024)}, u32[]{:S(2)}) copy-start(f32[2048]{0:T(1024)} %param.18) | copy-start | bytes 24580
Sparse Core Ops, SparseCore 0:
  42.0 52.7 all-gather.3
